TPU v7x, 256 devices: a whole 4x4x8 slice. The times are simulated.
256 devices in a mesh: row: 8 (over y, core), col: 32 (over x, z).
Axes of the slice: x: 4, y: 4, z: 8, core: 2. Of those that a mesh axis runs over, the one named last changes fastest.
Arguments:
- sources: float32 [65536, 256], P(('row', 'col')), may hold values from -6 to 6
- targets: float32 [65536, 256], P(('col', 'row')), may hold values from -6 to 6
- g_pot: float32 [65536], P(('col', 'row')), may hold values from -1 to 12
- log_a: float32 [65536], P(('row', 'col')), may hold values from -14 to -8
- log_b: float32 [65536], P(('col', 'row')), may hold values from -14 to -8
- src_block: int32 [16384], P(('row', 'col')), may hold values from 0 to 31, as said below
- tgt_block: int32 [16384], P(('row', 'col')), may hold values from 0 to 7, as said below
- pair_count: int32 [256], P(('row', 'col')), may hold values from 16 to 64, as said below
Outputs:
- f_new: float32 [65536], P(('row', 'col'))
- g_new: float32 [65536], P(('col', 'row'))
Inputs may be any that keep to these rules, and one draw needn't show every extreme that they name: `src_block`: within each row index, slot 0 of the 32 devices names together every source block of that row index once; slot k and slot k + 32 of a device name the same source block. `tgt_block`: within each col index, slot 0 of the 8 devices names together every target block of that col index once. `pair_count`: some device has all 64 slots live.
All inputs are finite; a program needn't handle non-finite values.
Results may differ from a plain program's by a relative error of at most 0.0003.
Values sent between devices are 32-bit elements; how exact they have to be, the bound alone decides.
A program may use at most 128 MiB of HBM per device.

v0:
```python
import jax
import jax.numpy as jnp
from jax import lax
from jax.sharding import PartitionSpec as P

BLK = 256
entropy = 0.05
lowest = -1e30


def squares_of(rows):
    return jnp.sum(rows * rows, axis=-1)


def cost_blocks(src_rows, tgt_rows, src_sq, tgt_sq):
    inner = jnp.einsum("kid,kjd->kij", src_rows, tgt_rows, precision=lax.Precision.HIGHEST)
    return (src_sq[:, :, None] + tgt_sq[:, None, :] - 2.0 * inner) / src_rows.shape[2]


def fold_blocks(slot_top, slot_total, slot_ids, alive, count):
    onehot = (slot_ids[:, None] == jnp.arange(count, dtype=jnp.int32)[None, :]) & alive[:, None]
    masked = jnp.where(onehot.T[:, :, None], slot_top[None, :, :], lowest)
    top = jnp.max(masked, axis=1)
    back = jnp.take(top, slot_ids, axis=0)
    weighted = jnp.where(alive[:, None], slot_total * jnp.exp(slot_top - back), 0.0)
    total = jnp.dot(onehot.T.astype(jnp.float32), weighted, precision=lax.Precision.HIGHEST)
    return (top.reshape(-1), total.reshape(-1))


def local(sources, targets, g_pot, log_a, log_b, src_block, tgt_block, pair_count):
    used_pairs = pair_count[0]
    slots = src_block.shape[0]
    alive = jnp.arange(slots, dtype=jnp.int32) < used_pairs
    tgt_all, pot_all = (
        lax.all_gather(targets, "row", axis=0, tiled=True),
        lax.all_gather(g_pot, "row", axis=0, tiled=True),
    )
    src_all, weight_all = (
        lax.all_gather(sources, "col", axis=0, tiled=True),
        lax.all_gather(log_a, "col", axis=0, tiled=True),
    )
    width = sources.shape[1]
    src_count = src_all.shape[0] // BLK
    tgt_count = tgt_all.shape[0] // BLK
    src_blocks = src_all.reshape(src_count, BLK, width)
    tgt_blocks = tgt_all.reshape(tgt_count, BLK, width)
    src_sq_all = squares_of(src_blocks)
    tgt_sq_all = squares_of(tgt_blocks)
    src_rows = jnp.take(src_blocks, src_block, axis=0)
    tgt_rows = jnp.take(tgt_blocks, tgt_block, axis=0)
    src_sq = jnp.take(src_sq_all, src_block, axis=0)
    tgt_sq = jnp.take(tgt_sq_all, tgt_block, axis=0)
    pot_rows = jnp.take(pot_all.reshape(tgt_count, BLK), tgt_block, axis=0)
    costs = cost_blocks(src_rows, tgt_rows, src_sq, tgt_sq)
    scores = (pot_rows[:, None, :] - costs) / entropy
    slot_top = jnp.max(scores, axis=2)
    slot_total = jnp.sum(jnp.exp(scores - slot_top[:, :, None]), axis=2)
    src_top, src_total = fold_blocks(slot_top, slot_total, src_block, alive, src_count)
    whole_top = lax.pmax(src_top, "col")
    src_total = lax.psum(src_total * jnp.exp(src_top - whole_top), "col")
    src_top = whole_top
    f_all = entropy * weight_all - entropy * (src_top + jnp.log(src_total))
    second_costs = cost_blocks(src_rows, tgt_rows, src_sq, tgt_sq)
    f_rows = jnp.take(f_all.reshape(src_count, BLK), src_block, axis=0)
    back_scores = (f_rows[:, :, None] - second_costs) / entropy
    col_top = jnp.max(back_scores, axis=1)
    col_total = jnp.sum(jnp.exp(back_scores - col_top[:, None, :]), axis=1)
    tgt_top, tgt_total = fold_blocks(col_top, col_total, tgt_block, alive, tgt_count)
    whole_tgt = lax.pmax(tgt_top, "row")
    tgt_total = lax.psum(tgt_total * jnp.exp(tgt_top - whole_tgt), "row")
    tgt_top = whole_tgt
    own_src = sources.shape[0]
    own_tgt = targets.shape[0]
    f_own = lax.dynamic_slice_in_dim(f_all, lax.axis_index("col") * own_src, own_src, 0)
    tgt_offset = lax.axis_index("row") * own_tgt
    top_own = lax.dynamic_slice_in_dim(tgt_top, tgt_offset, own_tgt, 0)
    total_own = lax.dynamic_slice_in_dim(tgt_total, tgt_offset, own_tgt, 0)
    g_own = entropy * log_b - entropy * (top_own + jnp.log(total_own))
    return (f_own, g_own)


def solution(mesh):
    placed = (
        P(("row", "col"), None),
        P(("col", "row"), None),
        P(("col", "row")),
        P(("row", "col")),
        P(("col", "row")),
        P(("row", "col")),
        P(("row", "col")),
        P(("row", "col")),
    )
    return jax.shard_map(
        local,
        mesh=mesh,
        in_specs=placed,
        out_specs=(P(("row", "col")), P(("col", "row"))),
        check_vma=False,
    )
```

profile of v0, /device:TPU:1, one launch (start us, length us, event | category | flops | bytes accessed | tf_op | source)
XLA Modules:
  0.0 527.1 jit_solution(1191801241612126786)
XLA Ops:
  7.2 0.7 all-gather.7.cloned.1.call-update
  7.9 0.7 all-gather.5.cloned.1.call-update
  8.7 12.4 %all-gather.1 = f32[8,1,256]{2,1,0:T(1,128)S(1)} all-gather(f32[1,1,256]{2,1,0:T(1,128)} %bitcast.32), channel_id=1, replica_groups=mesh['row'=8,'col'=32] {'row'}, dimensions={0}, use_global_device_ids=true | all-gather | bytes 9216 | tf_op jit(solution)/shard_map/all_gather | solution.py:36
  21.7 0.7 compare_select_fusion.1
  22.4 0.7 gather_fusion.2
  23.0 37.7 %all-gather = f32[32,1,256]{2,1,0:T(1,128)S(1)} all-gather(f32[1,1,256]{2,1,0:T(1,128)} %bitcast.33), channel_id=1, replica_groups=mesh['row'=8,'col'=32] {'col'}, dimensions={0}, use_global_device_ids=true | all-gather | bytes 33792 | tf_op jit(solution)/shard_map/all_gather | solution.py:40
  60.8 0.7 compare_select_fusion
  61.4 0.7 compare_and_fusion.1
  62.1 0.7 compare_and_fusion
  62.8 0.7 fusion.37
  63.4 0.7 fusion.36
  64.2 1.9 multiply_reduce_fusion.1
  66.1 0.7 gather_fusion.4
  66.8 10.5 %gather_fusion.1 = f32[64,256,256]{2,1,0:T(8,128)} fusion(f32[8,256,256]{2,1,0:T(8,128)} %bitcast.20, s32[1024]{0:T(1024)S(1)} %pad_clamp_fusion.1), kind=kCustom, calls=%fused_computation.7 | custom fusion | bytes 33554688 | tf_op jit(solution)/shard_map/jit(_take)/gather | solution.py:50
  77.3 64.3 %all-gather.5.cloned.1.call-done = f32[8192,256]{1,0:T(8,128)} async-done(((f32[256,256]{1,0:T(8,128)}), f32[8192,256]{1,0:T(8,128)}) %all-gather.5.cloned.1.call-update) | async-done | bytes 8388624 | tf_op jit(solution)/shard_map/all_gather | solution.py:39
  141.6 4.5 multiply_reduce_fusion
  146.2 0.7 gather_fusion.3
  146.8 11.6 %gather_fusion = f32[64,256,256]{2,1,0:T(8,128)} fusion(f32[32,256,256]{2,1,0:T(8,128)} %bitcast.21, s32[1024]{0:T(1024)S(1)} %pad_clamp_fusion), kind=kCustom, calls=%fused_computation.6 | custom fusion | bytes 33554688 | tf_op jit(solution)/shard_map/jit(_take)/gather | solution.py:49
  158.5 29.9 %fusion.3 = (f32[64,256]{1,0:T(8,128)S(1)}, f32[64,256,256]{2,1,0:T(8,128)}) fusion(f32[64,256]{1,0:T(8,128)S(1)} %get-tuple-element.4, f32[64,256,256]{2,1,0:T(8,128)} %gather_fusion.1, pred[64]{0:T(512)(128)(4,1)S(1)} %compare_and_fusion.1, f32[64,256,256]{2,1,0:T(8,128)} %gather_fusion, pred[64]{0:T(512)(128)(4,1)S(1)} %compare_and_fusion, ...), kind=kOutput, calls=%fused_computation.16 | convolution fusion | flops 12922634240 | bytes 50593920 | tf_op jit(solution)/shard_map/kid,kjd->kij/dot_general | solution.py:16
  188.4 8.5 %exponential_reduce_fusion.1 = f32[64,256]{1,0:T(8,128)S(1)} fusion(f32[64,256,256]{2,1,0:T(8,128)} %get-tuple-element.7, f32[64,256]{1,0:T(8,128)S(1)} %get-tuple-element.6, f32[64,256]{1,0:T(8,128)S(1)} %get-tuple-element.4), kind=kLoop, calls=%fused_computation.10 | loop fusion | flops 16760832 | bytes 16973824 | tf_op jit(solution)/shard_map/reduce_sum | solution.py:57
  197.0 0.5 select_reduce_fusion
  197.5 0.7 gather_fusion.5
  198.5 111.5 %pmax.14 = f32[8192]{0:T(1024)S(1)} all-reduce(f32[8192]{0:T(1024)S(1)} %bitcast.25), channel_id=1, replica_groups=mesh['row'=8,'col'=32] {'col'}, use_global_device_ids=true, to_apply=%region_4.7 | all-reduce | flops 8192 | bytes 65536 | tf_op jit(solution)/shard_map/pmax | solution.py:59
  310.0 110.7 %psum.14 = f32[8192]{0:T(1024)S(1)} all-reduce(f32[8192]{0:T(1024)S(1)} %exponential_multiply_fusion), channel_id=1, replica_groups=mesh['row'=8,'col'=32] {'col'}, use_global_device_ids=true, to_apply=%region_6.9 | all-reduce | flops 8192 | bytes 65536 | tf_op jit(solution)/shard_map/psum | solution.py:60
  420.8 0.7 gather_fusion.6
  421.5 7.2 %fusion.4 = f32[64,256]{1,0:T(8,128)S(1)} fusion(f32[64,256,256]{2,1,0:T(8,128)} %get-tuple-element.7, f32[64,256]{1,0:T(8,128)S(1)} %broadcast_select_fusion), kind=kLoop, calls=%fused_computation.17 | loop fusion | flops 12566528 | bytes 16908288 | tf_op jit(solution)/shard_map/reduce_max | solution.py:66
  428.8 8.0 %exponential_reduce_fusion = f32[64,256]{1,0:T(8,128)S(1)} fusion(f32[64,256,256]{2,1,0:T(8,128)} %get-tuple-element.7, f32[64,256]{1,0:T(8,128)S(1)} %fusion.4, f32[64,256]{1,0:T(8,128)S(1)} %broadcast_select_fusion), kind=kLoop, calls=%fused_computation.8 | loop fusion | flops 16760832 | bytes 16973824 | tf_op jit(solution)/shard_map/reduce_sum | solution.py:67
  437.0 0.7 gather_fusion.7
  437.9 68.4 %pmax.15 = f32[2048]{0:T(1024)S(1)} all-reduce(f32[2048]{0:T(1024)S(1)} %bitcast.29), channel_id=1, replica_groups=mesh['row'=8,'col'=32] {'row'}, use_global_device_ids=true, to_apply=%region_9.12 | all-reduce | flops 2048 | bytes 16384 | tf_op jit(solution)/shard_map/pmax | solution.py:69
  506.3 12.7 %psum.15 = f32[2048]{0:T(1024)S(1)} all-reduce(f32[2048]{0:T(1024)S(1)} %exponential_multiply_fusion.1), channel_id=1, replica_groups=mesh['row'=8,'col'=32] {'row'}, use_global_device_ids=true, to_apply=%region_11.14 | all-reduce | flops 2048 | bytes 16384 | tf_op jit(solution)/shard_map/psum | solution.py:70
  519.0 0.6 dynamic_slice.9
  519.7 0.6 multiply_subtract_fusion.1
  (30 shorter events, 1.2 us)
Async XLA Ops:
  7.2 57.0 %all-gather.7.cloned.1.call-start = ((), (), s32[]{:S(2)}) async-start(), calls=%async_computation.1 | async-start | bytes 2359296 | tf_op jit(solution)/shard_map/all_gather | solution.py:35
  7.9 133.7 %all-gather.5.cloned.1.call-start = ((), (), s32[]{:S(2)}) async-start(), calls=%async_computation | async-start | bytes 8650752 | tf_op jit(solution)/shard_map/all_gather | solution.py:39
  188.4 9.7 %copy-start.1 = (s32[64]{0:T(128)S(1)}, s32[64]{0:T(128)}, u32[]{:S(2)}) copy-start(s32[64]{0:T(128)} %param.17) | copy-start | bytes 772
  421.5 16.1 %copy-start.2 = (s32[64]{0:T(128)S(1)}, s32[64]{0:T(128)}, u32[]{:S(2)}) copy-start(s32[64]{0:T(128)} %param.18) | copy-start | bytes 772
  421.5 98.1 %copy-start = (f32[256]{0:T(256)S(1)}, f32[256]{0:T(256)}, u32[]{:S(2)}) copy-start(f32[256]{0:T(256)} %param.16) | copy-start | bytes 3076
Sparse Core Ops, SparseCore 0:
  9.8 32.0 all-gather.6
  44.5 97.0 all-gather.4
where the time goes:
time: 528 us; the launch traced here: 527 us
  blocking collectives  353 us (67%)
  waiting for transfers between devices  65.7 us (12%)
  other arithmetic  35.9 us (7%)
  matrix products  30.4 us (6%)
  local copies, waits for them, and re-layouts  26.8 us (5%)
  between operations  14.9 us (3%)
    pmax x1, blocking collectives, local(): whole_top = lax.pmax(src_top, 'col')  112 us
    psum x1, blocking collectives, local(): src_total = lax.psum(src_total * jnp.exp(src_top - whole_top), 'col')  111 us
    pmax x1, blocking collectives, local(): whole_tgt = lax.pmax(tgt_top, 'row')  68.4 us
    all_gather x1, waiting for transfers between devices, local(): lax.all_gather(sources, 'col', axis=0, tiled=True)  64.3 us
    all_gather x1, blocking collectives, local(): lax.all_gather(log_a, 'col', axis=0, tiled=True)  37.7 us
    dot_general x1, matrix products, cost_blocks(): jnp.einsum('kid,kjd->kij', src_rows, tgt_rows, precision=lax.Precision.HI...  29.9 us
    psum x1, blocking collectives, local(): tgt_total = lax.psum(tgt_total * jnp.exp(tgt_top - whole_tgt), 'row')  12.7 us
    all_gather x1, blocking collectives, local(): lax.all_gather(g_pot, 'row', axis=0, tiled=True)  12.4 us
  transfers between devices with their start and end apart: 2, of which 1 were waited for; matrix products, arithmetic and copies ran while one was open for 3% of the time, Pallas kernels for 0%

commit v1 on v0

--- a/solution.py
+++ b/solution.py
@@ -57,7 +57,7 @@
     slot_total = jnp.sum(jnp.exp(scores - slot_top[:, :, None]), axis=2)
     src_top, src_total = fold_blocks(slot_top, slot_total, src_block, alive, src_count)
     whole_top = lax.pmax(src_top, "col")
-    src_total = lax.psum(src_total * jnp.exp(src_top - whole_top), "col")
+    src_total = jnp.sum(lax.all_gather(src_total * jnp.exp(src_top - whole_top), "col"), axis=0)
     src_top = whole_top
     f_all = entropy * weight_all - entropy * (src_top + jnp.log(src_total))
     second_costs = cost_blocks(src_rows, tgt_rows, src_sq, tgt_sq)

time: 528 us -> 462 us (0.88)
  blocking collectives: 353 us -> 186 us
  waiting for transfers between devices: 65.7 us -> 167 us
    psum x1 -> x0, blocking collectives: 111 us -> none  [local(): src_total = lax.psum(src_total * jnp.exp(src_top - whole_top), 'col')]
    all_gather x0 -> x1, waiting for transfers between devices: none -> 62.3 us  [local(): lax.all_gather(src_total * jnp.exp(src_top - whole_top), 'col')]
    pmax x1, blocking collectives: 68.4 us -> 17.7 us  [local(): whole_tgt = lax.pmax(tgt_top, 'row')]
    all_gather x1, waiting for transfers between devices: 64.3 us -> 86.6 us  [local(): lax.all_gather(sources, 'col', axis=0, tiled=True)]
    all_gather x1, waiting for transfers between devices: 0.02 us -> 16.2 us  [local(): lax.all_gather(targets, 'row', axis=0, tiled=True)]
    all_gather x1, blocking collectives: 37.7 us -> 31.2 us  [local(): lax.all_gather(log_a, 'col', axis=0, tiled=True)]
  transfers between devices with their start and end apart: 2 -> 3, of which waited for: 1 -> 3; matrix products, arithmetic and copies ran while one was open for 3% -> 4% of each run, Pallas kernels for 0% -> 0%
where the time goes in v1:
time: 462 us; the launch traced here: 461 us
  blocking collectives  186 us (40%)
  waiting for transfers between devices  167 us (36%)
  other arithmetic  35.9 us (8%)
  matrix products  30.5 us (7%)
  local copies, waits for them, and re-layouts  28.1 us (6%)
  between operations  14.6 us (3%)
    pmax x1, blocking collectives, local(): whole_top = lax.pmax(src_top, 'col')  112 us
    all_gather x1, waiting for transfers between devices, local(): lax.all_gather(sources, 'col', axis=0, tiled=True)  86.6 us
    all_gather x1, waiting for transfers between devices, local(): lax.all_gather(src_total * jnp.exp(src_top - whole_top), 'col')  62.3 us
    all_gather x1, blocking collectives, local(): lax.all_gather(log_a, 'col', axis=0, tiled=True)  31.2 us
    dot_general x1, matrix products, cost_blocks(): jnp.einsum('kid,kjd->kij', src_rows, tgt_rows, precision=lax.Precision.HI...  29.9 us
    pmax x1, blocking collectives, local(): whole_tgt = lax.pmax(tgt_top, 'row')  17.7 us
    all_gather x1, waiting for transfers between devices, local(): lax.all_gather(targets, 'row', axis=0, tiled=True)  16.2 us
    psum x1, blocking collectives, local(): tgt_total = lax.psum(tgt_total * jnp.exp(tgt_top - whole_tgt), 'row')  12.7 us
  transfers between devices with their start and end apart: 3, of which 3 were waited for; matrix products, arithmetic and copies ran while one was open for 4% of the time, Pallas kernels for 0%

profile of v1, /device:TPU:1, one launch (start us, length us, event | category | flops | bytes accessed | tf_op | source)
XLA Modules:
  0.0 461.3 jit_solution(2991369276296060857)
XLA Ops:
  7.2 0.7 all-gather.9.cloned.1.call-update
  7.9 0.7 all-gather.7.cloned.1.call-update
  8.7 12.4 %all-gather.2 = f32[8,1,256]{2,1,0:T(1,128)S(1)} all-gather(f32[1,1,256]{2,1,0:T(1,128)} %bitcast.32), channel_id=1, replica_groups=mesh['row'=8,'col'=32] {'row'}, dimensions={0}, use_global_device_ids=true | all-gather | bytes 9216 | tf_op jit(solution)/shard_map/all_gather | solution.py:36
  21.7 0.7 compare_select_fusion.1
  22.4 0.7 gather_fusion.2
  23.1 0.7 compare_select_fusion
  23.7 0.7 compare_and_fusion.1
  24.4 0.7 compare_and_fusion
  25.1 0.7 fusion.36
  25.7 16.2 %all-gather.9.cloned.1.call-done = f32[2048,256]{1,0:T(8,128)} async-done(((f32[256,256]{1,0:T(8,128)}), f32[2048,256]{1,0:T(8,128)}) %all-gather.9.cloned.1.call-update) | async-done | bytes 2097168 | tf_op jit(solution)/shard_map/all_gather | solution.py:35
  41.9 1.9 multiply_reduce_fusion.1
  43.9 0.7 gather_fusion.4
  44.5 10.4 %gather_fusion.1 = f32[64,256,256]{2,1,0:T(8,128)} fusion(f32[8,256,256]{2,1,0:T(8,128)} %bitcast.20, s32[1024]{0:T(1024)S(1)} %pad_clamp_fusion.1), kind=kCustom, calls=%fused_computation.7 | custom fusion | bytes 33554688 | tf_op jit(solution)/shard_map/jit(_take)/gather | solution.py:50
  55.0 86.6 %all-gather.7.cloned.1.call-done = f32[8192,256]{1,0:T(8,128)} async-done(((f32[256,256]{1,0:T(8,128)}), f32[8192,256]{1,0:T(8,128)}) %all-gather.7.cloned.1.call-update) | async-done | bytes 8388624 | tf_op jit(solution)/shard_map/all_gather | solution.py:39
  141.6 4.5 multiply_reduce_fusion
  146.2 0.7 gather_fusion.3
  146.8 11.6 %gather_fusion = f32[64,256,256]{2,1,0:T(8,128)} fusion(f32[32,256,256]{2,1,0:T(8,128)} %bitcast.21, s32[1024]{0:T(1024)S(1)} %pad_clamp_fusion), kind=kCustom, calls=%fused_computation.6 | custom fusion | bytes 33554688 | tf_op jit(solution)/shard_map/jit(_take)/gather | solution.py:49
  158.5 29.9 %fusion.3 = (f32[64,256]{1,0:T(8,128)S(1)}, f32[64,256,256]{2,1,0:T(8,128)}) fusion(f32[64,256]{1,0:T(8,128)S(1)} %get-tuple-element.4, f32[64,256,256]{2,1,0:T(8,128)} %gather_fusion.1, pred[64]{0:T(512)(128)(4,1)S(1)} %compare_and_fusion.1, f32[64,256,256]{2,1,0:T(8,128)} %gather_fusion, pred[64]{0:T(512)(128)(4,1)S(1)} %compare_and_fusion, ...), kind=kOutput, calls=%fused_computation.16 | convolution fusion | flops 12922634240 | bytes 50593920 | tf_op jit(solution)/shard_map/kid,kjd->kij/dot_general | solution.py:16
  188.5 8.6 %exponential_reduce_fusion.1 = f32[64,256]{1,0:T(8,128)S(1)} fusion(f32[64,256,256]{2,1,0:T(8,128)} %get-tuple-element.7, f32[64,256]{1,0:T(8,128)S(1)} %get-tuple-element.6, f32[64,256]{1,0:T(8,128)S(1)} %get-tuple-element.4), kind=kLoop, calls=%fused_computation.10 | loop fusion | flops 16760832 | bytes 16973824 | tf_op jit(solution)/shard_map/reduce_sum | solution.py:57
  197.5 0.7 gather_fusion.5
  198.6 111.5 %pmax.14 = f32[8192]{0:T(1024)S(1)} all-reduce(f32[8192]{0:T(1024)S(1)} %bitcast.25), channel_id=1, replica_groups=mesh['row'=8,'col'=32] {'col'}, use_global_device_ids=true, to_apply=%region_4.7 | all-reduce | flops 8192 | bytes 65536 | tf_op jit(solution)/shard_map/pmax | solution.py:59
  310.7 31.2 %all-gather.1 = f32[32,1,256]{2,1,0:T(1,128)S(1)} all-gather(f32[1,1,256]{2,1,0:T(1,128)S(1)} %bitcast.33), channel_id=1, replica_groups=mesh['row'=8,'col'=32] {'col'}, dimensions={0}, use_global_device_ids=true | all-gather | bytes 33792 | tf_op jit(solution)/shard_map/all_gather | solution.py:40
  342.0 62.3 %all-gather.11.cloned.1.call-done = f32[262144]{0:T(1024)} async-done(((f32[8192]{0:T(1024)}), f32[262144]{0:T(1024)}) %all-gather.11.cloned.1.call-update) | async-done | bytes 1048592 | tf_op jit(solution)/shard_map/all_gather | solution.py:60
  404.3 1.4 reshape.194
  405.9 0.7 gather_fusion.6
  406.6 7.2 %fusion.4 = f32[64,256]{1,0:T(8,128)S(1)} fusion(f32[64,256,256]{2,1,0:T(8,128)} %get-tuple-element.7, f32[64,256]{1,0:T(8,128)S(1)} %broadcast_select_fusion), kind=kLoop, calls=%fused_computation.17 | loop fusion | flops 12566528 | bytes 16908288 | tf_op jit(solution)/shard_map/reduce_max | solution.py:66
  413.9 8.0 %exponential_reduce_fusion = f32[64,256]{1,0:T(8,128)S(1)} fusion(f32[64,256,256]{2,1,0:T(8,128)} %get-tuple-element.7, f32[64,256]{1,0:T(8,128)S(1)} %fusion.4, f32[64,256]{1,0:T(8,128)S(1)} %broadcast_select_fusion), kind=kLoop, calls=%fused_computation.8 | loop fusion | flops 16760832 | bytes 16973824 | tf_op jit(solution)/shard_map/reduce_sum | solution.py:67
  422.1 0.7 gather_fusion.7
  423.0 17.7 %pmax.15 = f32[2048]{0:T(1024)S(1)} all-reduce(f32[2048]{0:T(1024)S(1)} %bitcast.29), channel_id=1, replica_groups=mesh['row'=8,'col'=32] {'row'}, use_global_device_ids=true, to_apply=%region_9.12 | all-reduce | flops 2048 | bytes 16384 | tf_op jit(solution)/shard_map/pmax | solution.py:69
  440.8 12.7 %psum.7 = f32[2048]{0:T(1024)S(1)} all-reduce(f32[2048]{0:T(1024)S(1)} %exponential_multiply_fusion.1), channel_id=1, replica_groups=mesh['row'=8,'col'=32] {'row'}, use_global_device_ids=true, to_apply=%region_11.14 | all-reduce | flops 2048 | bytes 16384 | tf_op jit(solution)/shard_map/psum | solution.py:70
  453.4 0.6 dynamic_slice.9
  454.1 0.6 multiply_subtract_fusion.1
  (36 shorter events, 2.5 us)
Async XLA Ops:
  7.2 34.8 %all-gather.9.cloned.1.call-start = ((), (), s32[]{:S(2)}) async-start(), calls=%async_computation.1 | async-start | bytes 2359296 | tf_op jit(solution)/shard_map/all_gather | solution.py:35
  7.9 133.7 %all-gather.7.cloned.1.call-start = ((), (), s32[]{:S(2)}) async-start(), calls=%async_computation | async-start | bytes 8650752 | tf_op jit(solution)/shard_map/all_gather | solution.py:39
  8.6 395.7 %all-gather.11.cloned.1.call-start = ((), (), s32[]{:S(2)}) async-start(), calls=%async_computation.2 | async-start | bytes 1081344 | tf_op jit(solution)/shard_map/all_gather | solution.py:60
  188.4 9.8 %copy-start.2 = (s32[64]{0:T(128)S(1)}, s32[64]{0:T(128)}, u32[]{:S(2)}) copy-start(s32[64]{0:T(128)} %param.17) | copy-start | bytes 772
  188.4 122.3 %copy-start = (f32[256]{0:T(256)S(1)}, f32[256]{0:T(256)}, u32[]{:S(2)}) copy-start(f32[256]{0:T(256)} %param.15) | copy-start | bytes 3076
  188.4 153.5 %copy-start.3 = (s32[64]{0:T(128)S(1)}, s32[64]{0:T(128)}, u32[]{:S(2)}) copy-start(s32[64]{0:T(128)} %param.18) | copy-start | bytes 772
  406.6 47.5 %copy-start.1 = (f32[256]{0:T(256)S(1)}, f32[256]{0:T(256)}, u32[]{:S(2)}) copy-start(f32[256]{0:T(256)} %param.16) | copy-start | bytes 3076
Sparse Core Ops, SparseCore 0:
  9.8 32.0 all-gather.8
  44.5 97.0 all-gather.6
  310.8 93.4 all-gather.10
